TPU v7x, 512 devices: a whole 4x8x8 slice. The times are simulated.
512 devices in a mesh: aux: 8 (over z), ao: 16 (over y, core), orb: 4 (over x).
Axes of the slice: x: 4, y: 8, z: 8, core: 2. Of those that a mesh axis runs over, the one named last changes fastest.
Arguments:
- integrals: bfloat16 [128, 16, 4, 128, 128], P('aux', 'ao', None, 'orb'), may hold values from -6 to 6
- partner: int32 [16, 4], P('ao'), may hold values from 0 to 15
- pair_count: int32 [16], P('ao'), may hold values from 1 to 4
- occupied_coeff: bfloat16 [2048, 512], P('ao', 'orb'), may hold values from -0.25 to 0.25
- occupied_domain: int32 [16, 4], P('ao', 'orb'), may hold values 0 or 1
- virtual_coeff: bfloat16 [2048, 8192], P('aux', 'ao'), may hold values from -0.125 to 0.125
- virtual_domain: int32 [16, 64], P(None, 'ao'), may hold values 0 or 1
Outputs:
- transformed: bfloat16 [128, 512, 8192], P('aux', 'orb', 'ao')
All inputs are finite; a program needn't handle non-finite values. No bound on the sum of `occupied_domain` or of `virtual_domain` on one device may be relied on, other than what follows from the above.
Results may differ from a plain program's by a relative error of at most 0.0049.
Values may be sent and summed in bfloat16 or wider, within the bound.
A program may use at most 64 MiB of HBM per device.

v0:
```python
import jax
import jax.numpy as jnp
from jax import lax
from jax.sharding import PartitionSpec as P


def local(
    integrals, partner, pair_count, occupied_coeff, occupied_domain, virtual_coeff, virtual_domain
):
    block_size = integrals.shape[4]
    slab_rows = integrals.shape[0]
    local_blocks = integrals.shape[1]
    slot_count = integrals.shape[2]
    occ_width = occupied_coeff.shape[1]
    domain_wire = occupied_domain.astype(jnp.bfloat16)
    all_occ, all_domain = (
        lax.all_gather(occupied_coeff, "ao", axis=0, tiled=True),
        lax.all_gather(domain_wire, "ao", axis=0, tiled=True),
    )
    occ_mask = jnp.repeat(jnp.repeat(all_domain, block_size, axis=0), block_size, axis=1)
    occ_masked = all_occ * occ_mask
    block_total = all_domain.shape[0]
    picked = occ_masked.reshape(block_total, block_size, occ_width)[partner]
    slots = jnp.arange(slot_count, dtype=jnp.int32)
    live = (slots[None, :] < pair_count[:, None]).astype(jnp.bfloat16)
    picked = picked * live[:, :, None, None]
    all_columns = lax.all_to_all(picked, "orb", split_axis=2, concat_axis=3, tiled=True)
    partial_term = jnp.einsum(
        "nkri,pnkrv->pinv", all_columns, integrals, preferred_element_type=jnp.float32
    )
    half_wide = lax.psum_scatter(partial_term, "orb", scatter_dimension=1, tiled=True)
    half_local = half_wide.reshape(slab_rows, occ_width, local_blocks * block_size).astype(
        jnp.bfloat16
    )
    vir_rows = lax.all_gather(virtual_coeff, "aux", axis=0, tiled=True)
    vir_mask = jnp.repeat(
        jnp.repeat(virtual_domain, block_size, axis=0), block_size, axis=1
    ).astype(jnp.bfloat16)
    vir_masked = vir_rows * vir_mask
    vir_width = vir_masked.shape[1]
    piece = lax.all_gather(half_local, "ao", axis=2, tiled=True)
    count = piece.shape[2]
    flat = piece.reshape(slab_rows * occ_width, count)
    product = jnp.dot(flat, vir_masked, preferred_element_type=jnp.float32)
    result = product.reshape(slab_rows, occ_width, vir_width)
    return result.astype(jnp.bfloat16)


def solution(mesh):
    placed = (
        P("aux", "ao", None, "orb", None),
        P("ao", None),
        P("ao"),
        P("ao", "orb"),
        P("ao", "orb"),
        P("aux", "ao"),
        P(None, "ao"),
    )
    return jax.shard_map(
        local, mesh=mesh, in_specs=placed, out_specs=P("aux", "orb", "ao"), check_vma=False
    )
```

profile of v0, /device:TPU:1, one launch (start us, length us, event | category | flops | bytes accessed | tf_op | source)
XLA Modules:
  0.0 215.5 jit_solution(4892264346600140509)
XLA Ops:
  7.4 0.0 copy-start
  7.4 0.0 reduce-scatter.2.cloned.1.call-start
  8.7 0.7 fusion.11
  9.4 1.3 dynamic-slice
  10.7 0.7 dynamic-update-slice
  11.3 29.8 %all-reduce = bf16[16]{0:T(256)(128)(2,1)S(1)} all-reduce(bf16[16]{0:T(256)(128)(2,1)S(1)} %dynamic-update-slice), channel_id=1, replica_groups=mesh['aux'=8,'ao'=16,'orb'=4] {'ao'}, use_global_device_ids=true, to_apply=%add | all-reduce | flops 16 | bytes 64
  41.1 0.1 broadcast_bitcast_fusion
  41.2 16.4 %all_gather.14 = bf16[2048,128]{1,0:T(8,128)(2,1)S(1)} all-gather(bf16[128,128]{1,0:T(8,128)(2,1)} %param.10), channel_id=1, replica_groups=mesh['aux'=8,'ao'=16,'orb'=4] {'ao'}, dimensions={0}, use_global_device_ids=true | all-gather | bytes 557056 | tf_op jit(solution)/shard_map/all_gather | solution.py:17
  57.6 0.3 broadcast_multiply_fusion
  58.0 0.6 gather_fusion
  58.5 0.1 bitcast_multiply_fusion.1
  58.6 0.1 copy.14
  58.7 7.3 %all_to_all.15 = bf16[1,4,128,128]{3,1,0,2:T(4,128)(2,1)S(1)} all-to-all(bf16[1,4,128,128]{3,1,0,2:T(4,128)(2,1)S(1)} %copy.14), channel_id=1, replica_groups=mesh['aux'=8,'ao'=16,'orb'=4] {'orb'}, dimensions={2} | all-to-all | bytes 262144 | tf_op jit(solution)/shard_map/all_to_all | solution.py:27
  66.1 0.1 copy.16
  66.1 0.1 reshape.70
  66.2 0.0 copy-done
  66.2 2.7 %convolution_bitcast_fusion = f32[16,512,1,128]{3,1,0,2:T(8,128)} fusion(bf16[4,32,512,1]{2,1,0,3:T(8,128)(2,1)S(1)} %reshape.70, bf16[16,1,4,32,128]{4,3,2,1,0:T(8,128)(2,1)S(1)} %copy-done), kind=kOutput, calls=%fused_computation.3 | convolution fusion | flops 268435456 | bytes 4849664 | tf_op jit(solution)/shard_map/nkri,pnkrv->pinv/dot_general | solution.py:28
  68.9 0.0 reduce-scatter.2.cloned.1.call-update
  68.9 0.0 copy-start.1
  68.9 0.0 all-gather.4.cloned.1.call-start
  69.0 0.5 all-gather.4.cloned.1.call-update
  69.5 0.0 all-gather.6.cloned.1.call-start
  69.6 51.7 %reduce-scatter.2.cloned.1.call-done = f32[16,128,1,128]{3,1,0,2:T(8,128)} async-done(((f32[16,512,1,128]{3,1,0,2:T(8,128)}), f32[16,128,1,128]{3,1,0,2:T(8,128)}) %reduce-scatter.2.cloned.1.call-update) | async-done | bytes 1048592 | tf_op jit(solution)/shard_map/reduce_scatter | solution.py:31
  121.2 2.1 convert_element_type.34
  123.3 0.0 all-gather.6.cloned.1.call-update
  123.4 0.0 copy-done.1
  123.4 0.1 copy.17
  123.5 0.0 all-gather.4.cloned.1.call-done
  123.5 0.0 copy-start.2
  123.5 69.4 %all-gather.6.cloned.1.call-done = bf16[16,128,1,2048]{3,1,0,2:T(8,128)(2,1)} async-done(((bf16[16,128,1,128]{3,1,0,2:T(8,128)(2,1)}), bf16[16,128,1,2048]{3,1,0,2:T(8,128)(2,1)}) %all-gather.6.cloned.1.call-update) | async-done | bytes 8388624 | tf_op jit(solution)/shard_map/all_gather | solution.py:41
  192.9 0.1 broadcast_in_dim.21
  193.0 5.8 %broadcast_in_dim.22 = bf16[2048,4,128]{2,1,0:T(4,128)(2,1)S(1)} broadcast(bf16[2048,4]{1,0:T(8,128)(2,1)S(1)} %bitcast.47), dimensions={0,1} | broadcast | bytes 2113536 | tf_op jit(solution)/shard_map/broadcast_in_dim | solution.py:36
  198.7 0.0 copy-done.2
  198.8 9.3 %fusion.5 = bf16[16,128,512]{2,1,0:T(8,128)(2,1)} fusion(bf16[2048,512]{1,0:T(8,128)(2,1)S(1)} %copy-done.2, bf16[256,8,4,128]{3,2,1,0:T(4,128)(2,1)S(1)} %bitcast.46, bf16[16,128,1,2048]{3,1,0,2:T(8,128)(2,1)} %all-gather.6.cloned.1.call-done), kind=kOutput, calls=%fused_computation.7 | convolution fusion | flops 4297064448 | bytes 14680064 | tf_op jit(solution)/shard_map/dot_general | solution.py:44
  (5 shorter events, 0.0 us)
Async XLA Ops:
  7.4 58.8 %copy-start = (bf16[16,1,4,32,128]{4,3,2,1,0:T(8,128)(2,1)S(1)}, bf16[16,1,4,32,128]{4,3,2,1,0:T(8,128)(2,1)}, u32[]{:S(2)}) copy-start(bf16[16,1,4,32,128]{4,3,2,1,0:T(8,128)(2,1)} %param.7) | copy-start | bytes 1572868
  7.4 113.9 %reduce-scatter.2.cloned.1.call-start = ((), (), s32[]{:S(2)}) async-start(), calls=%async_computation.2 | async-start | bytes 5242880 | tf_op jit(solution)/shard_map/reduce_scatter | solution.py:31
  68.9 54.5 %copy-start.1 = (s32[16,4]{0,1:T(4,128)S(1)}, s32[16,4]{0,1:T(4,128)}, u32[]{:S(2)}) copy-start(s32[16,4]{0,1:T(4,128)} %param.13) | copy-start | bytes 772
  68.9 54.6 %all-gather.4.cloned.1.call-start = ((), (), s32[]{:S(2)}) async-start(), calls=%async_computation.3 | async-start | bytes 2359296 | tf_op jit(solution)/shard_map/all_gather | solution.py:35
  69.5 123.4 %all-gather.6.cloned.1.call-start = ((), (), s32[]{:S(2)}) async-start(), calls=%async_computation.4 | async-start | bytes 8912896 | tf_op jit(solution)/shard_map/all_gather | solution.py:41
  123.5 75.3 %copy-start.2 = (bf16[2048,512]{1,0:T(8,128)(2,1)S(1)}, bf16[2048,512]{1,0:T(8,128)(2,1)}, u32[]{:S(2)}) copy-start(bf16[2048,512]{1,0:T(8,128)(2,1)} %all-gather.4.cloned.1.call-done) | copy-start | bytes 6291460
Sparse Core Ops, SparseCore 0:
  69.0 52.1 reduce-scatter.1
Sparse Core Ops, SparseCore 1:
  71.5 40.2 all-gather.3
  123.5 69.4 all-gather.5
where the time goes:
time: 216 us
  waiting for transfers between devices  122 us (56%)
  blocking collectives  53.5 us (25%)
  between operations  16.3 us (8%)
  matrix products  12 us (6%)
  local copies, waits for them, and re-layouts  8.79 us (4%)
  other arithmetic  3.2 us (1%)
    all_gather x1, waiting for transfers between devices, local(): piece = lax.all_gather(half_local, 'ao', axis=2, tiled=True)  69.4 us
    reduce_scatter x1, waiting for transfers between devices, local(): lax.psum_scatter(partial_term, 'orb', scatter_dimension=1, tiled=True)  51.7 us
    unnamed x1, blocking collectives  29.8 us
    all_gather x1, blocking collectives, local(): lax.all_gather(occupied_coeff, 'ao', axis=0, tiled=True)  16.4 us
    dot_general x1, matrix products, local(): product = jnp.dot(flat, vir_masked, preferred_element_type=jnp.float32)  9.32 us
    all_to_all x1, blocking collectives, local(): lax.all_to_all(picked, 'orb', split_axis=2, concat_axis=3, tiled=True)  7.31 us
    broadcast_in_dim x1, local copies, waits for them, and re-layouts, local(): jnp.repeat(jnp.repeat(virtual_domain, block_size, axis=0), block_size, ax...  5.78 us
  transfers between devices with their start and end apart: 3, of which 2 were waited for; matrix products, arithmetic and copies ran while one was open for 1% of the time, Pallas kernels for 0%

commit v1 on v0

v1 whole, which is shorter than its diff:
```python
import jax
import jax.numpy as jnp
from jax import lax
from jax.sharding import PartitionSpec as P


def local(
    integrals, partner, pair_count, occupied_coeff, occupied_domain, virtual_coeff, virtual_domain
):
    block_size = integrals.shape[4]
    slab_rows = integrals.shape[0]
    slot_count = integrals.shape[2]
    occ_width = occupied_coeff.shape[1]
    occ_local = occupied_coeff * occupied_domain.astype(jnp.bfloat16)
    all_occ = lax.all_gather(occ_local, "ao", axis=0, tiled=True)
    all_ints = lax.all_gather(integrals, "orb", axis=3, tiled=True)

    vir_blocks = virtual_coeff.shape[0] // block_size
    first = lax.axis_index("aux") * vir_blocks
    dom = lax.dynamic_slice_in_dim(virtual_domain, first, vir_blocks, axis=0).astype(jnp.bfloat16)
    dom = jnp.repeat(jnp.repeat(dom, block_size, axis=0), block_size, axis=1)
    vir_masked = lax.all_gather(virtual_coeff * dom, "aux", axis=0, tiled=True)

    picked = all_occ.reshape(-1, block_size, occ_width)[partner[0]]
    slots = jnp.arange(slot_count, dtype=jnp.int32)
    live = (slots < pair_count[0]).astype(jnp.bfloat16)
    picked = picked * live[:, None, None]
    half = jnp.einsum(
        "kri,pkrv->piv", picked, all_ints[:, 0], preferred_element_type=jnp.float32
    ).astype(jnp.bfloat16)
    piece = lax.all_gather(half, "ao", axis=2, tiled=True)
    flat = piece.reshape(slab_rows * occ_width, piece.shape[2])
    product = jnp.dot(flat, vir_masked, preferred_element_type=jnp.float32)
    return product.reshape(slab_rows, occ_width, -1).astype(jnp.bfloat16)


def solution(mesh):
    placed = (
        P("aux", "ao", None, "orb", None),
        P("ao", None),
        P("ao"),
        P("ao", "orb"),
        P("ao", "orb"),
        P("aux", "ao"),
        P(None, "ao"),
    )
    return jax.shard_map(
        local, mesh=mesh, in_specs=placed, out_specs=P("aux", "orb", "ao"), check_vma=False
    )
```

time: 216 us -> 184 us (0.85)
  blocking collectives: 53.5 us -> 22.4 us
  local copies, waits for them, and re-layouts: 8.79 us -> 1.02 us
  waiting for transfers between devices: 122 us -> 129 us
    all_gather x2 -> x3, waiting for transfers between devices: 69.4 us -> 128 us  [the longest x1 74.3 us: local(): piece = lax.all_gather(half, 'ao', axis=2, tiled=True)]
    reduce_scatter x1 -> x0, waiting for transfers between devices: 51.7 us -> none  [local(): lax.psum_scatter(partial_term, 'orb', scatter_dimension=1, tiled=True)]
    unnamed x1 -> x0, blocking collectives: 29.8 us -> none
    all_to_all x1 -> x0, blocking collectives: 7.31 us -> none  [local(): lax.all_to_all(picked, 'orb', split_axis=2, concat_axis=3, tiled=True)]
    all_gather x1, blocking collectives: 16.4 us -> 22.4 us  [local(): all_occ = lax.all_gather(occ_local, 'ao', axis=0, tiled=True)]
    broadcast_in_dim x3 -> x2, local copies, waits for them, and re-layouts: 5.93 us -> 0.34 us  [local(): dom = jnp.repeat(jnp.repeat(dom, block_size, axis=0), block_size, axis=1)]
  transfers between devices with their start and end apart: 3 -> 3, of which waited for: 2 -> 3; matrix products, arithmetic and copies ran while one was open for 1% -> 4% of each run, Pallas kernels for 0% -> 0%
where the time goes in v1:
time: 184 us
  waiting for transfers between devices  129 us (70%)
  blocking collectives  22.4 us (12%)
  between operations  14.4 us (8%)
  matrix products  12.7 us (7%)
  other arithmetic  3.9 us (2%)
    all_gather x1, waiting for transfers between devices, local(): piece = lax.all_gather(half, 'ao', axis=2, tiled=True)  74.3 us
    all_gather x1, waiting for transfers between devices, local(): vir_masked = lax.all_gather(virtual_coeff * dom, 'aux', axis=0, tiled=True)  39.3 us
    all_gather x1, blocking collectives, local(): all_occ = lax.all_gather(occ_local, 'ao', axis=0, tiled=True)  22.4 us
    all_gather x1, waiting for transfers between devices, local(): all_ints = lax.all_gather(integrals, 'orb', axis=3, tiled=True)  14.8 us
    dot_general x1, matrix products, local(): product = jnp.dot(flat, vir_masked, preferred_element_type=jnp.float32)  9.82 us
  transfers between devices with their start and end apart: 3, of which 3 were waited for; matrix products, arithmetic and copies ran while one was open for 4% of the time, Pallas kernels for 0%

profile of v1, /device:TPU:1, one launch (start us, length us, event | category | flops | bytes accessed | tf_op | source)
XLA Modules:
  0.0 183.8 jit_solution(8361173918025073191)
XLA Ops:
  6.5 0.0 all-gather.4.cloned.1.call-start
  6.5 0.7 all-gather.4.cloned.1.call-update
  7.3 0.0 all-gather.8.cloned.1.call-start
  7.3 0.8 dynamic-slice_convert_fusion
  8.1 0.1 copy.8
  8.2 0.3 broadcast_in_dim.9
  8.5 1.7 bitcast_multiply_fusion
  10.2 0.0 all-gather.8.cloned.1.call-update
  10.3 0.0 all-gather.6.cloned.1.call-start
  11.6 0.7 fusion.19
  12.3 0.8 broadcast_multiply_fusion
  13.0 22.4 %all_gather.12 = bf16[2048,128]{1,0:T(8,128)(2,1)S(1)} all-gather(bf16[128,128]{1,0:T(8,128)(2,1)S(1)} %broadcast_multiply_fusion), channel_id=1, replica_groups=mesh['aux'=8,'ao'=16,'orb'=4] {'ao'}, dimensions={0}, use_global_device_ids=true | all-gather | bytes 557056 | tf_op jit(solution)/shard_map/all_gather | solution.py:15
  35.4 0.6 gather_fusion
  36.0 14.8 %all-gather.4.cloned.1.call-done = bf16[16,1,4,128,128]{4,3,2,1,0:T(8,128)(2,1)} async-done(((bf16[16,1,4,32,128]{4,3,2,1,0:T(8,128)(2,1)}), bf16[16,1,4,128,128]{4,3,2,1,0:T(8,128)(2,1)}) %all-gather.4.cloned.1.call-update) | async-done | bytes 2097168 | tf_op jit(solution)/shard_map/all_gather | solution.py:16
  50.9 2.9 %fusion.13 = bf16[16,128,128]{2,1,0:T(8,128)(2,1)} fusion(bf16[16,1,4,128,128]{4,3,2,1,0:T(8,128)(2,1)} %all-gather.4.cloned.1.call-done, bf16[4,128,128]{2,1,0:T(8,128)(2,1)S(1)} %gather_fusion, bf16[4]{0:T(256)(128)(2,1)S(1)} %compare_convert_fusion), kind=kOutput, calls=%fused_computation.8 | convolution fusion | flops 268959744 | bytes 2752520 | tf_op jit(solution)/shard_map/kri,pkrv->piv/dot_general | solution.py:28
  53.8 0.0 all-gather.6.cloned.1.call-update
  53.8 39.3 %all-gather.8.cloned.1.call-done = bf16[2048,512]{1,0:T(8,128)(2,1)} async-done(((bf16[256,512]{1,0:T(8,128)(2,1)}), bf16[2048,512]{1,0:T(8,128)(2,1)}) %all-gather.8.cloned.1.call-update) | async-done | bytes 2097168 | tf_op jit(solution)/shard_map/all_gather | solution.py:22
  93.1 74.3 %all-gather.6.cloned.1.call-done = bf16[16,128,2048]{2,1,0:T(8,128)(2,1)} async-done(((bf16[16,128,128]{2,1,0:T(8,128)(2,1)}), bf16[16,128,2048]{2,1,0:T(8,128)(2,1)}) %all-gather.6.cloned.1.call-update) | async-done | bytes 8388624 | tf_op jit(solution)/shard_map/all_gather | solution.py:31
  167.4 9.8 %fusion.4 = bf16[16,128,512]{2,1,0:T(8,128)(2,1)} fusion(bf16[16,128,2048]{2,1,0:T(8,128)(2,1)} %all-gather.6.cloned.1.call-done, bf16[2048,512]{1,0:T(8,128)(2,1)} %all-gather.8.cloned.1.call-done), kind=kOutput, calls=%fused_computation.5 | convolution fusion | flops 4296015872 | bytes 12582912 | tf_op jit(solution)/shard_map/dot_general | solution.py:33
  (3 shorter events, 0.0 us)
Async XLA Ops:
  6.5 44.3 %all-gather.4.cloned.1.call-start = ((), (), s32[]{:S(2)}) async-start(), calls=%async_computation | async-start | bytes 2621440 | tf_op jit(solution)/shard_map/all_gather | solution.py:16
  7.3 85.9 %all-gather.8.cloned.1.call-start = ((), (), s32[]{:S(2)}) async-start(), calls=%async_computation.2 | async-start | bytes 2359296 | tf_op jit(solution)/shard_map/all_gather | solution.py:22
  10.3 157.2 %all-gather.6.cloned.1.call-start = ((), (), s32[]{:S(2)}) async-start(), calls=%async_computation.1 | async-start | bytes 8912896 | tf_op jit(solution)/shard_map/all_gather | solution.py:31
Sparse Core Ops, SparseCore 0:
  9.4 41.3 all-gather.3
  52.9 40.1 all-gather.7
  95.2 72.2 all-gather.5

commit v2 on v1

v2 whole, which is shorter than its diff:
```python
import functools

import jax
import jax.numpy as jnp
from jax import lax
from jax.experimental import pallas as pl
from jax.experimental.pallas import tpu as pltpu
from jax.sharding import PartitionSpec as P

MESH = pl.DeviceIdType.MESH
CHUNKS = 4


class Keys:
    def __init__(self):
        self.index = {}

    def __getitem__(self, key):
        return self.index.setdefault(key, len(self.index))


def kernel(
    size, chunks, occ, ints, vir, partner, count, vdom, out,
    occ_all, from_left, from_right, from_far, spread, half, vir_all, vir_masked, staged,
    send_sem, recv_sem, out_sem,
):
    nz, ny, nx = size
    slab, slots, rows, width = ints.shape
    per = slab // chunks
    keys = Keys()
    pending = []

    z, me, x = lax.axis_index("aux"), lax.axis_index("ao"), lax.axis_index("orb")
    y, core = me // 2, me % 2
    sibling = {"ao": y * 2 + 1 - core}

    def around(axis, delta):
        if axis == "aux":
            return {"aux": (z + delta + nz) % nz}
        if axis == "orb":
            return {"orb": (x + delta + nx) % nx}
        return {"ao": ((y + delta + ny) % ny) * 2 + core}

    def block(delta, same=True):
        return ((y + delta + ny) % ny) * 2 + (core if same else 1 - core)

    def copy(key, src, dst, device):
        i = keys[key]
        return pltpu.make_async_remote_copy(
            src_ref=src, dst_ref=dst, send_sem=send_sem.at[i], recv_sem=recv_sem.at[i],
            device_id=device, device_id_type=MESH,
        )

    def post(key, src, dst, device):
        c = copy(key, src, dst, device)
        c.start()
        pending.append(c)

    def arrive(key, dst, device=sibling):
        copy(key, dst, dst, device).wait_recv()

    barrier = pltpu.get_barrier_semaphore()
    peers = [around("orb", 1), around("orb", -1), around("aux", 1), around("aux", -1), sibling]
    peers += [around("ao", d) for d in range(1, ny)]
    for peer in peers:
        pl.semaphore_signal(barrier, inc=1, device_id=peer, device_id_type=MESH)
    pl.semaphore_wait(barrier, len(peers))

    def part(c):
        return pl.ds(c * per, per)

    def ints_own(c):
        post(("x", "R", c), ints.at[part(c)], from_left.at[part(c)], around("orb", 1))
        post(("x", "L", c), ints.at[part(c)], from_right.at[part(c)], around("orb", -1))

    def ints_step(c):
        arrive(("x", "R", c), from_left.at[part(c)])
        arrive(("x", "L", c), from_right.at[part(c)])
        if c % 2 == 0:
            post(("x", "D", c), from_left.at[part(c)], from_far.at[part(c)], around("orb", 1))
        else:
            post(("x", "D", c), from_right.at[part(c)], from_far.at[part(c)], around("orb", -1))
        if c + 2 < chunks:
            ints_own(c + 2)

    ints_own(0)
    for d in (1, 7, 2, 6, 3, 5, 4):
        post(("o", d), occ, occ_all.at[me], around("ao", d))
    post(("os", 0), occ, occ_all.at[me], sibling)
    ints_own(1)
    for h in range(2):
        post(("v", "R", 1, h), vir.at[h], vir_all.at[z * 2 + h], around("aux", 1))
        post(("v", "L", 1, h), vir.at[h], vir_all.at[z * 2 + h], around("aux", -1))
    occ_all[me] = occ[...]
    for h in range(2):
        vir_all[z * 2 + h] = vir[h]

    ints_step(0)
    for d in (1, 7, 2, 6, 3, 5, 4):
        slot = occ_all.at[block(-d)]
        arrive(("o", d), slot)
        post(("os", d), slot, slot, sibling)
    for d in (0, 1, 7, 2, 6, 3, 5, 4):
        arrive(("os", d), occ_all.at[block(-d, False)])

    pieces = []
    for rel in (0, -1, 1, 2):
        first = pl.multiple_of(((x + rel + nx) % nx) * rows, rows)
        for k in range(slots):
            live = jnp.where(k < count[0], 1.0, 0.0).astype(jnp.float32)
            picked = occ_all[partner[0, k], pl.ds(first, rows), :].astype(jnp.float32)
            pieces.append(picked * live)
    spread[...] = jnp.concatenate(pieces, axis=0).T.astype(jnp.bfloat16)

    def half_step(c):
        arrive(("x", "D", c), from_far.at[part(c)])
        columns = []
        for p in range(c * per, (c + 1) * per):
            columns.append(
                jnp.concatenate(
                    [
                        ref[p].reshape(slots * rows, width)
                        for ref in (ints, from_left, from_right, from_far)
                    ],
                    axis=0,
                )
            )
        res = jnp.dot(
            spread[...], jnp.concatenate(columns, axis=1), preferred_element_type=jnp.float32
        ).astype(jnp.bfloat16)
        for j in range(per):
            half[me, c * per + j] = res[:, j * width : (j + 1) * width]
        own = half.at[me, part(c)]
        post(("y", "R", 1, c), own, own, around("ao", 1))
        post(("y", "L", 1, c), own, own, around("ao", -1))
        post(("s", "O", 0, c), own, own, sibling)

    def routes(d, c):
        far = ny // 2
        if d < far:
            return ("R", "L")
        if d > far:
            return ()
        return ("R",) if c % 2 == 0 else ("L",)

    def half_pass(d, c):
        for way in routes(d, c):
            sign = 1 if way == "R" else -1
            slot = half.at[block(-sign * d), part(c)]
            arrive(("y", way, d, c), slot)
            if way in routes(d + 1, c):
                post(("y", way, d + 1, c), slot, slot, around("ao", sign))
            post(("s", way, d, c), slot, slot, sibling)

    def vir_pass(d):
        for h in range(2):
            for way in routes(d, h):
                sign = 1 if way == "R" else -1
                slot = vir_all.at[((z - sign * d + nz) % nz) * 2 + h]
                arrive(("v", way, d, h), slot)
                if way in routes(d + 1, h):
                    post(("v", way, d + 1, h), slot, slot, around("aux", sign))

    def mask():
        def body(m, carry):
            for b in range(vdom.shape[1]):
                on = jnp.full((width, width), vdom[m, b].astype(jnp.float32)).astype(jnp.bfloat16)
                at = slice(b * width, (b + 1) * width)
                first = pl.multiple_of(m * width, width)
                vir_masked[pl.ds(first, width), at] = vir_all[m, :, at] * on
            return carry

        lax.fori_loop(0, vir_all.shape[0], body, 0)

    def drain(c):
        arrive(("s", "O", 0, c), half.at[block(0, False), part(c)])
        for d in range(1, ny // 2 + 1):
            for way in routes(d, c):
                sign = 1 if way == "R" else -1
                arrive(("s", way, d, c), half.at[block(-sign * d, False), part(c)])

    def multiply(c):
        blocks = half.shape[0]

        def body(t, carry):
            p = c * per + t * 2
            lhs = jnp.concatenate(
                [half[n, pl.ds(p, 2)].reshape(2 * width, width) for n in range(blocks)], axis=1
            )
            res = jnp.dot(lhs, vir_masked[...], preferred_element_type=jnp.float32)
            staged[pl.ds(p, 2)] = res.astype(jnp.bfloat16).reshape(2, width, -1)
            return carry

        lax.fori_loop(0, per // 2, body, 0)
        done = pltpu.make_async_copy(staged.at[part(c)], out.at[part(c)], out_sem.at[c])
        done.start()
        return done

    outs = []
    far = ny // 2
    for s in range(chunks + far):
        if s + 1 < chunks:
            ints_step(s + 1)
        if s < chunks:
            half_step(s)
        if s < far:
            vir_pass(s + 1)
        for d in range(1, far + 1):
            if 0 <= s - d < chunks:
                half_pass(d, s - d)
        if s == far:
            mask()
        if s >= far:
            drain(s - far)
            outs.append(multiply(s - far))
    for c in pending:
        c.wait_send()
    for c in outs:
        c.wait()


def copies(chunks):
    return 18 * chunks + 29


def local(size, integrals, partner, pair_count, occ_coeff, occ_domain, vir_coeff, vir_domain):
    slab, _, slots, rows, width = integrals.shape
    nz, ny, nx = size
    blocks = 2 * ny
    occ_width = occ_coeff.shape[1]
    vir_width = vir_coeff.shape[1]
    occ = occ_coeff * occ_domain.astype(jnp.bfloat16)
    ints = integrals.reshape(slab, slots, rows, width)
    vir = vir_coeff.reshape(-1, width, vir_width)
    n = copies(CHUNKS)
    vmem = pl.BlockSpec(memory_space=pltpu.VMEM)
    smem = pl.BlockSpec(memory_space=pltpu.SMEM)
    return pl.pallas_call(
        functools.partial(kernel, size, CHUNKS),
        out_shape=jax.ShapeDtypeStruct((slab, occ_width, vir_width), jnp.bfloat16),
        in_specs=[vmem] * 3 + [smem] * 3,
        out_specs=pl.BlockSpec(memory_space=pl.ANY),
        scratch_shapes=[
            pltpu.VMEM((blocks, width, occ_width), jnp.bfloat16),
            pltpu.VMEM(ints.shape, jnp.bfloat16),
            pltpu.VMEM(ints.shape, jnp.bfloat16),
            pltpu.VMEM(ints.shape, jnp.bfloat16),
            pltpu.VMEM((occ_width, nx * slots * rows), jnp.bfloat16),
            pltpu.VMEM((blocks, slab, occ_width, width), jnp.bfloat16),
            pltpu.VMEM((blocks, width, vir_width), jnp.bfloat16),
            pltpu.VMEM((blocks * width, vir_width), jnp.bfloat16),
            pltpu.VMEM((slab, occ_width, vir_width), jnp.bfloat16),
            pltpu.SemaphoreType.DMA((n,)),
            pltpu.SemaphoreType.DMA((n,)),
            pltpu.SemaphoreType.DMA((CHUNKS,)),
        ],
        compiler_params=pltpu.CompilerParams(
            collective_id=0, has_side_effects=True, vmem_limit_bytes=60 * 1024 * 1024
        ),
    )(occ, ints, vir, partner, pair_count, vir_domain)


def solution(mesh):
    size = (mesh.shape["aux"], mesh.shape["ao"] // 2, mesh.shape["orb"])
    placed = (
        P("aux", "ao", None, "orb", None),
        P("ao", None),
        P("ao"),
        P("ao", "orb"),
        P("ao", "orb"),
        P("aux", "ao"),
        P(None, "ao"),
    )
    return jax.shard_map(
        functools.partial(local, size), mesh=mesh, in_specs=placed,
        out_specs=P("aux", "orb", "ao"), check_vma=False,
    )
```

time: 184 us -> 86.9 us (0.47)
  waiting for transfers between devices: 129 us -> 0 us
  Pallas kernels: 0 us -> 79.5 us
  blocking collectives: 22.4 us -> 0 us
  between operations: 14.4 us -> 1.31 us
  matrix products: 12.7 us -> 0 us
  local copies, waits for them, and re-layouts: 1.02 us -> 4.45 us
  other arithmetic: 3.9 us -> 1.38 us
    all_gather x3 -> x0, waiting for transfers between devices: 128 us -> none  [the longest x1 74.3 us: local(): piece = lax.all_gather(half, 'ao', axis=2, tiled=True)]
    pallas_call x0 -> x1, Pallas kernels: none -> 79.5 us  [local(): pl.pallas_call(functools.partial(kernel, size, CHUNKS), out_shape=jax.Sha...]
    all_gather x1 -> x0, blocking collectives: 22.4 us -> none  [local(): all_occ = lax.all_gather(occ_local, 'ao', axis=0, tiled=True)]
    dot_general x2 -> x0, matrix products: 12.7 us -> none  [the longest x1 9.82 us: local(): product = jnp.dot(flat, vir_masked, preferred_element_type=jnp.float32)]
    unnamed x0 -> x2, local copies, waits for them, and re-layouts: none -> 4.45 us
  transfers between devices with their start and end apart: 3 -> 0, of which waited for: 3 -> 0; matrix products, arithmetic and copies ran while one was open for 4% -> 0% of each run, Pallas kernels for 0% -> 0%
where the time goes in v2:
time: 86.9 us; the launch traced here: 86.7 us
  Pallas kernels  79.5 us (91%)
  local copies, waits for them, and re-layouts  4.45 us (5%)
  other arithmetic  1.38 us (2%)
  between operations  1.31 us (2%)
    pallas_call x1, Pallas kernels, local(): pl.pallas_call(functools.partial(kernel, size, CHUNKS), out_shape=jax.Sha...  79.5 us
    unnamed x2, local copies, waits for them, and re-layouts  4.45 us

profile of v2, /device:TPU:1, one launch (start us, length us, event | category | flops | bytes accessed | tf_op | source)
XLA Modules:
  0.0 86.7 jit_solution(14216806257652910736)
XLA Ops:
  1.3 1.4 %copy.8.vdom = s32[16,4]{1,0:T(8,128)} copy(s32[16,4]{0,1:T(4,128)} %param.13) | data formatting | bytes 512 | tf_op args[6]
  2.7 1.4 %broadcast_multiply_fusion.occ = bf16[128,128]{1,0:T(8,128)(2,1)} fusion(bf16[128,128]{1,0:T(8,128)(2,1)} %param.10, bf16[]{:T(256)} %bitcast), kind=kLoop, calls=%fused_computation | loop fusion | flops 16384 | bytes 65538 | tf_op jit(solution)/shard_map/mul | solution.py:232
  4.0 79.5 %shard_map.73 = bf16[16,128,512]{2,1,0:T(8,128)(2,1)} custom-call(bf16[128,128]{1,0:T(8,128)(2,1)} %broadcast_multiply_fusion.occ, bf16[16,4,32,128]{3,2,1,0:T(8,128)(2,1)} %bitcast.3, bf16[2,128,512]{2,1,0:T(8,128)(2,1)} %bitcast.4, s32[1,4]{1,0:T(1,128)} %partner.1, s32[1]{0:T(128)S(6)} %copy.10.count, s32[16,4]{1,0:T(8,128)} %copy.8.vdom), custom_call_target="tpu_custom_call" | custom-call | tf_op jit(solution)/shard_map/pallas_call | solution.py:238
  83.6 3.1 %copy.12 = bf16[16,128,512]{2,1,0:T(8,128)(2,1)} copy(bf16[16,128,512]{2,1,0:T(8,128)(2,1)} %shard_map.73) | data formatting | bytes 4194304

commit v3 on v2

--- a/solution.py
+++ b/solution.py
@@ -8,7 +8,8 @@
 from jax.sharding import PartitionSpec as P
 
 MESH = pl.DeviceIdType.MESH
-CHUNKS = 4
+CHUNKS = (4, 4, 4, 4)
+VIR_STEPS = (1, 2, 3, 4)
 
 
 class Keys:
@@ -20,13 +21,14 @@
 
 
 def kernel(
-    size, chunks, occ, ints, vir, partner, count, vdom, out,
+    size, sizes, vir_steps, occ, ints, vir, partner, count, odom, vdom, out,
     occ_all, from_left, from_right, from_far, spread, half, vir_all, vir_masked, staged,
     send_sem, recv_sem, out_sem,
 ):
     nz, ny, nx = size
     slab, slots, rows, width = ints.shape
-    per = slab // chunks
+    chunks = len(sizes)
+    firsts = [sum(sizes[:c]) for c in range(chunks)]
     keys = Keys()
     pending = []
 
@@ -59,6 +61,11 @@
     def arrive(key, dst, device=sibling):
         copy(key, dst, dst, device).wait_recv()
 
+    keep = jnp.full(occ.shape, odom[0, 0].astype(jnp.float32)).astype(jnp.bfloat16)
+    occ_all[me] = occ[...] * keep
+    for h in range(2):
+        vir_all[z * 2 + h] = vir[h]
+
     barrier = pltpu.get_barrier_semaphore()
     peers = [around("orb", 1), around("orb", -1), around("aux", 1), around("aux", -1), sibling]
     peers += [around("ao", d) for d in range(1, ny)]
@@ -67,7 +74,7 @@
     pl.semaphore_wait(barrier, len(peers))
 
     def part(c):
-        return pl.ds(c * per, per)
+        return pl.ds(firsts[c], sizes[c])
 
     def ints_own(c):
         post(("x", "R", c), ints.at[part(c)], from_left.at[part(c)], around("orb", 1))
@@ -85,21 +92,19 @@
 
     ints_own(0)
     for d in (1, 7, 2, 6, 3, 5, 4):
-        post(("o", d), occ, occ_all.at[me], around("ao", d))
-    post(("os", 0), occ, occ_all.at[me], sibling)
+        post(("o", d), occ_all.at[me], occ_all.at[me], around("ao", d))
+    post(("os", 0), occ_all.at[me], occ_all.at[me], sibling)
     ints_own(1)
     for h in range(2):
         post(("v", "R", 1, h), vir.at[h], vir_all.at[z * 2 + h], around("aux", 1))
         post(("v", "L", 1, h), vir.at[h], vir_all.at[z * 2 + h], around("aux", -1))
-    occ_all[me] = occ[...]
-    for h in range(2):
-        vir_all[z * 2 + h] = vir[h]
 
     ints_step(0)
     for d in (1, 7, 2, 6, 3, 5, 4):
         slot = occ_all.at[block(-d)]
         arrive(("o", d), slot)
         post(("os", d), slot, slot, sibling)
+    ints_step(1)
     for d in (0, 1, 7, 2, 6, 3, 5, 4):
         arrive(("os", d), occ_all.at[block(-d, False)])
 
@@ -115,7 +120,7 @@
     def half_step(c):
         arrive(("x", "D", c), from_far.at[part(c)])
         columns = []
-        for p in range(c * per, (c + 1) * per):
+        for p in range(firsts[c], firsts[c] + sizes[c]):
             columns.append(
                 jnp.concatenate(
                     [
@@ -128,8 +133,8 @@
         res = jnp.dot(
             spread[...], jnp.concatenate(columns, axis=1), preferred_element_type=jnp.float32
         ).astype(jnp.bfloat16)
-        for j in range(per):
-            half[me, c * per + j] = res[:, j * width : (j + 1) * width]
+        for j in range(sizes[c]):
+            half[me, firsts[c] + j] = res[:, j * width : (j + 1) * width]
         own = half.at[me, part(c)]
         post(("y", "R", 1, c), own, own, around("ao", 1))
         post(("y", "L", 1, c), own, own, around("ao", -1))
@@ -163,8 +168,8 @@
 
     def mask():
         def body(m, carry):
-            for b in range(vdom.shape[1]):
-                on = jnp.full((width, width), vdom[m, b].astype(jnp.float32)).astype(jnp.bfloat16)
+            for b in range(vdom.shape[0]):
+                on = jnp.full((width, width), vdom[b, m].astype(jnp.float32)).astype(jnp.bfloat16)
                 at = slice(b * width, (b + 1) * width)
                 first = pl.multiple_of(m * width, width)
                 vir_masked[pl.ds(first, width), at] = vir_all[m, :, at] * on
@@ -183,7 +188,7 @@
         blocks = half.shape[0]
 
         def body(t, carry):
-            p = c * per + t * 2
+            p = firsts[c] + t * 2
             lhs = jnp.concatenate(
                 [half[n, pl.ds(p, 2)].reshape(2 * width, width) for n in range(blocks)], axis=1
             )
@@ -191,7 +196,7 @@
             staged[pl.ds(p, 2)] = res.astype(jnp.bfloat16).reshape(2, width, -1)
             return carry
 
-        lax.fori_loop(0, per // 2, body, 0)
+        lax.fori_loop(0, sizes[c] // 2, body, 0)
         done = pltpu.make_async_copy(staged.at[part(c)], out.at[part(c)], out_sem.at[c])
         done.start()
         return done
@@ -199,20 +204,22 @@
     outs = []
     far = ny // 2
     for s in range(chunks + far):
-        if s + 1 < chunks:
+        if 1 < s + 1 < chunks:
             ints_step(s + 1)
         if s < chunks:
             half_step(s)
-        if s < far:
-            vir_pass(s + 1)
         for d in range(1, far + 1):
             if 0 <= s - d < chunks:
                 half_pass(d, s - d)
-        if s == far:
+        for d in range(1, far + 1):
+            if s == vir_steps[d - 1]:
+                vir_pass(d)
+        if s == vir_steps[-1]:
             mask()
-        if s >= far:
-            drain(s - far)
-            outs.append(multiply(s - far))
+        if s >= max(far, vir_steps[-1]):
+            while len(outs) <= s - far:
+                drain(len(outs))
+                outs.append(multiply(len(outs)))
     for c in pending:
         c.wait_send()
     for c in outs:
@@ -229,16 +236,15 @@
     blocks = 2 * ny
     occ_width = occ_coeff.shape[1]
     vir_width = vir_coeff.shape[1]
-    occ = occ_coeff * occ_domain.astype(jnp.bfloat16)
     ints = integrals.reshape(slab, slots, rows, width)
     vir = vir_coeff.reshape(-1, width, vir_width)
-    n = copies(CHUNKS)
+    n = copies(len(CHUNKS))
     vmem = pl.BlockSpec(memory_space=pltpu.VMEM)
     smem = pl.BlockSpec(memory_space=pltpu.SMEM)
     return pl.pallas_call(
-        functools.partial(kernel, size, CHUNKS),
+        functools.partial(kernel, size, CHUNKS, VIR_STEPS),
         out_shape=jax.ShapeDtypeStruct((slab, occ_width, vir_width), jnp.bfloat16),
-        in_specs=[vmem] * 3 + [smem] * 3,
+        in_specs=[vmem] * 3 + [smem] * 4,
         out_specs=pl.BlockSpec(memory_space=pl.ANY),
         scratch_shapes=[
             pltpu.VMEM((blocks, width, occ_width), jnp.bfloat16),
@@ -252,12 +258,12 @@
             pltpu.VMEM((slab, occ_width, vir_width), jnp.bfloat16),
             pltpu.SemaphoreType.DMA((n,)),
             pltpu.SemaphoreType.DMA((n,)),
-            pltpu.SemaphoreType.DMA((CHUNKS,)),
+            pltpu.SemaphoreType.DMA((len(CHUNKS),)),
         ],
         compiler_params=pltpu.CompilerParams(
-            collective_id=0, has_side_effects=True, vmem_limit_bytes=60 * 1024 * 1024
+            collective_id=0, has_side_effects=True, vmem_limit_bytes=30 * 1024 * 1024
         ),
-    )(occ, ints, vir, partner, pair_count, vir_domain)
+    )(occ_coeff, ints, vir, partner, pair_count, occ_domain, vir_domain.T)
 
 
 def solution(mesh):

time: 86.9 us -> 81.7 us (0.940)
  Pallas kernels: 79.5 us -> 74.7 us
  other arithmetic: 1.38 us -> 0 us
  local copies, waits for them, and re-layouts: 4.45 us -> 5.4 us
    pallas_call x1, Pallas kernels: 79.5 us -> 74.7 us  [local(): pl.pallas_call(functools.partial(kernel, size, CHUNKS, VIR_STEPS), out_sh...]
    mul x1 -> x0, other arithmetic: 1.38 us -> none  [local(): occ = occ_coeff * occ_domain.astype(jnp.bfloat16)]
    unnamed x2 -> x11, local copies, waits for them, and re-layouts: 4.45 us -> 5.4 us
where the time goes in v3:
time: 81.7 us; the launch traced here: 81.4 us
  Pallas kernels  74.7 us (91%)
  local copies, waits for them, and re-layouts  5.4 us (7%)
  between operations  1.32 us (2%)
    pallas_call x1, Pallas kernels, local(): pl.pallas_call(functools.partial(kernel, size, CHUNKS, VIR_STEPS), out_sh...  74.7 us
    unnamed x11, local copies, waits for them, and re-layouts  5.4 us

profile of v3, /device:TPU:1, one launch (start us, length us, event | category | flops | bytes accessed | tf_op | source)
XLA Modules:
  0.0 81.4 jit_solution(3820958886189372271)
XLA Ops:
  1.3 0.0 copy-start
  1.3 1.0 %copy-done = bf16[16,1,4,32,128]{4,3,2,1,0:T(8,128)(2,1)S(1)} copy-done((bf16[16,1,4,32,128]{4,3,2,1,0:T(8,128)(2,1)S(1)}, bf16[16,1,4,32,128]{4,3,2,1,0:T(8,128)(2,1)}, u32[]{:S(2)}) %copy-start) | copy-done | bytes 524312
  2.3 0.0 copy-start.1
  2.3 0.9 %copy-done.1 = bf16[256,512]{1,0:T(8,128)(2,1)S(1)} copy-done((bf16[256,512]{1,0:T(8,128)(2,1)S(1)}, bf16[256,512]{1,0:T(8,128)(2,1)}, u32[]{:S(2)}) %copy-start.1) | copy-done | bytes 262168
  3.3 0.0 copy-start.2
  3.3 0.8 copy-done.2
  4.0 0.0 copy-start.3
  4.1 0.7 copy-done.3
  4.7 0.0 copy-start.4
  4.7 0.7 copy-done.4
  5.4 74.7 %shard_map.73 = bf16[16,128,512]{2,1,0:T(8,128)(2,1)S(1)} custom-call(bf16[128,128]{1,0:T(8,128)(2,1)S(1)} %copy-done.2, bf16[16,4,32,128]{3,2,1,0:T(8,128)(2,1)S(1)} %bitcast.3, bf16[2,128,512]{2,1,0:T(8,128)(2,1)S(1)} %bitcast.4, s32[1,4]{1,0:T(1,128)S(1)} %copy-done.4, s32[1]{0:T(128)S(6)} %copy.9.count, s32[1,1]{1,0:T(1,128)S(6)} %copy.10.odom, ...), custom_call_target="tpu_custom_call" | custom-call | tf_op jit(solution)/shard_map/pallas_call | solution.py:244
  80.1 1.3 %copy.11 = bf16[16,128,512]{2,1,0:T(8,128)(2,1)} copy(bf16[16,128,512]{2,1,0:T(8,128)(2,1)S(1)} %shard_map.73) | data formatting | bytes 4194304
Async XLA Ops:
  1.3 1.0 %copy-start = (bf16[16,1,4,32,128]{4,3,2,1,0:T(8,128)(2,1)S(1)}, bf16[16,1,4,32,128]{4,3,2,1,0:T(8,128)(2,1)}, u32[]{:S(2)}) copy-start(bf16[16,1,4,32,128]{4,3,2,1,0:T(8,128)(2,1)} %param.7) | copy-start | bytes 1572868
  2.3 0.9 %copy-start.1 = (bf16[256,512]{1,0:T(8,128)(2,1)S(1)}, bf16[256,512]{1,0:T(8,128)(2,1)}, u32[]{:S(2)}) copy-start(bf16[256,512]{1,0:T(8,128)(2,1)} %param.12) | copy-start | bytes 786436
  3.3 0.8 copy-start.2
  4.0 0.7 copy-start.3
  4.7 0.7 copy-start.4

commit v4 on v3

--- a/solution.py
+++ b/solution.py
@@ -22,7 +22,7 @@
 
 def kernel(
     size, sizes, vir_steps, occ, ints, vir, partner, count, odom, vdom, out,
-    occ_all, from_left, from_right, from_far, spread, half, vir_all, vir_masked, staged,
+    occ_all, from_left, from_right, from_far, spread, half, vir_all, vir_masked, staged, total,
     send_sem, recv_sem, out_sem,
 ):
     nz, ny, nx = size
@@ -177,9 +177,10 @@
 
         lax.fori_loop(0, vir_all.shape[0], body, 0)
 
-    def drain(c):
-        arrive(("s", "O", 0, c), half.at[block(0, False), part(c)])
-        for d in range(1, ny // 2 + 1):
+    def drain(c, near=True, last=True):
+        if near:
+            arrive(("s", "O", 0, c), half.at[block(0, False), part(c)])
+        for d in range(1 if near else ny // 2, ny // 2 + (1 if last else 0)):
             for way in routes(d, c):
                 sign = 1 if way == "R" else -1
                 arrive(("s", way, d, c), half.at[block(-sign * d, False), part(c)])
@@ -193,6 +194,42 @@
                 [half[n, pl.ds(p, 2)].reshape(2 * width, width) for n in range(blocks)], axis=1
             )
             res = jnp.dot(lhs, vir_masked[...], preferred_element_type=jnp.float32)
+            staged[pl.ds(p, 2)] = res.astype(jnp.bfloat16).reshape(2, width, -1)
+            return carry
+
+        lax.fori_loop(0, sizes[c] // 2, body, 0)
+        done = pltpu.make_async_copy(staged.at[part(c)], out.at[part(c)], out_sem.at[c])
+        done.start()
+        return done
+
+    def pair(delta, p):
+        there = (y + delta + ny) % ny
+        lhs = [half[there * 2 + n, pl.ds(p, 2)].reshape(2 * width, width) for n in range(2)]
+        rows_at = pl.multiple_of(there * 2 * width, 2 * width)
+        return lhs, vir_masked[pl.ds(rows_at, 2 * width), :]
+
+    def multiply_near(c):
+        def body(t, carry):
+            lhs, rhs = [], []
+            for delta in range(1 - ny // 2, ny // 2):
+                a, b = pair(delta, firsts[c] + t * 2)
+                lhs += a
+                rhs.append(b)
+            total[t] = jnp.dot(
+                jnp.concatenate(lhs, axis=1), jnp.concatenate(rhs, axis=0),
+                preferred_element_type=jnp.float32,
+            )
+            return carry
+
+        lax.fori_loop(0, sizes[c] // 2, body, 0)
+
+    def multiply_far(c):
+        def body(t, carry):
+            p = firsts[c] + t * 2
+            lhs, rhs = pair(ny // 2, p)
+            res = total[t] + jnp.dot(
+                jnp.concatenate(lhs, axis=1), rhs, preferred_element_type=jnp.float32
+            )
             staged[pl.ds(p, 2)] = res.astype(jnp.bfloat16).reshape(2, width, -1)
             return carry
 
@@ -218,8 +255,15 @@
             mask()
         if s >= max(far, vir_steps[-1]):
             while len(outs) <= s - far:
-                drain(len(outs))
-                outs.append(multiply(len(outs)))
+                if len(outs) == chunks - 1:
+                    drain(chunks - 1, near=False)
+                    outs.append(multiply_far(chunks - 1))
+                else:
+                    drain(len(outs))
+                    outs.append(multiply(len(outs)))
+        if s == chunks + far - 2:
+            drain(chunks - 1, last=False)
+            multiply_near(chunks - 1)
     for c in pending:
         c.wait_send()
     for c in outs:
@@ -256,6 +300,7 @@
             pltpu.VMEM((blocks, width, vir_width), jnp.bfloat16),
             pltpu.VMEM((blocks * width, vir_width), jnp.bfloat16),
             pltpu.VMEM((slab, occ_width, vir_width), jnp.bfloat16),
+            pltpu.VMEM((CHUNKS[-1] // 2, 2 * width, vir_width), jnp.float32),
             pltpu.SemaphoreType.DMA((n,)),
             pltpu.SemaphoreType.DMA((n,)),
             pltpu.SemaphoreType.DMA((len(CHUNKS),)),

time: 81.7 us -> 82.1 us (level)
  no operation moved by 1% of the time
where the time goes in v4:
time: 82.1 us; the launch traced here: 81.8 us
  Pallas kernels  75 us (91%)
  local copies, waits for them, and re-layouts  5.4 us (7%)
  between operations  1.32 us (2%)
    pallas_call x1, Pallas kernels, local(): pl.pallas_call(functools.partial(kernel, size, CHUNKS, VIR_STEPS), out_sh...  75 us
    unnamed x11, local copies, waits for them, and re-layouts  5.4 us

profile of v4, /device:TPU:1, one launch (start us, length us, event | category | flops | bytes accessed | tf_op | source)
XLA Modules:
  0.0 81.8 jit_solution(2621430994023478091)
XLA Ops:
  1.3 0.0 copy-start
  1.3 1.0 %copy-done = bf16[16,1,4,32,128]{4,3,2,1,0:T(8,128)(2,1)S(1)} copy-done((bf16[16,1,4,32,128]{4,3,2,1,0:T(8,128)(2,1)S(1)}, bf16[16,1,4,32,128]{4,3,2,1,0:T(8,128)(2,1)}, u32[]{:S(2)}) %copy-start) | copy-done | bytes 524312
  2.3 0.0 copy-start.1
  2.3 0.9 %copy-done.1 = bf16[256,512]{1,0:T(8,128)(2,1)S(1)} copy-done((bf16[256,512]{1,0:T(8,128)(2,1)S(1)}, bf16[256,512]{1,0:T(8,128)(2,1)}, u32[]{:S(2)}) %copy-start.1) | copy-done | bytes 262168
  3.3 0.0 copy-start.2
  3.3 0.8 copy-done.2
  4.0 0.0 copy-start.3
  4.1 0.7 copy-done.3
  4.7 0.0 copy-start.4
  4.7 0.7 copy-done.4
  5.4 75.0 %shard_map.73 = bf16[16,128,512]{2,1,0:T(8,128)(2,1)S(1)} custom-call(bf16[128,128]{1,0:T(8,128)(2,1)S(1)} %copy-done.2, bf16[16,4,32,128]{3,2,1,0:T(8,128)(2,1)S(1)} %bitcast.3, bf16[2,128,512]{2,1,0:T(8,128)(2,1)S(1)} %bitcast.4, s32[1,4]{1,0:T(1,128)S(1)} %copy-done.4, s32[1]{0:T(128)S(6)} %copy.9.count, s32[1,1]{1,0:T(1,128)S(6)} %copy.10.odom, ...), custom_call_target="tpu_custom_call" | custom-call | tf_op jit(solution)/shard_map/pallas_call | solution.py:288
  80.4 1.3 %copy.11 = bf16[16,128,512]{2,1,0:T(8,128)(2,1)} copy(bf16[16,128,512]{2,1,0:T(8,128)(2,1)S(1)} %shard_map.73) | data formatting | bytes 4194304
Async XLA Ops:
  1.3 1.0 %copy-start = (bf16[16,1,4,32,128]{4,3,2,1,0:T(8,128)(2,1)S(1)}, bf16[16,1,4,32,128]{4,3,2,1,0:T(8,128)(2,1)}, u32[]{:S(2)}) copy-start(bf16[16,1,4,32,128]{4,3,2,1,0:T(8,128)(2,1)} %param.7) | copy-start | bytes 1572868
  2.3 0.9 %copy-start.1 = (bf16[256,512]{1,0:T(8,128)(2,1)S(1)}, bf16[256,512]{1,0:T(8,128)(2,1)}, u32[]{:S(2)}) copy-start(bf16[256,512]{1,0:T(8,128)(2,1)} %param.12) | copy-start | bytes 786436
  3.3 0.8 copy-start.2
  4.0 0.7 copy-start.3
  4.7 0.7 copy-start.4
